TPU v7x, 32 devices: a whole 2x2x4 slice. The times are simulated.
32 devices in a mesh: doc: 2 (over core), coarse: 2 (over x), fine: 8 (over z, y).
Axes of the slice: x: 2, y: 2, z: 4, core: 2. Of those that a mesh axis runs over, the one named last changes fastest.
Arguments:
- q_light: bfloat16 [2, 2048, 1024], P('doc', ('coarse', 'fine')), may hold values from -8 to 8
- k_light: bfloat16 [2, 2048, 1024], P('doc', ('coarse', 'fine')), may hold values from -8 to 8
- v_light: bfloat16 [2, 2048, 1024], P('doc', ('coarse', 'fine')), may hold values from -6 to 6
- q_heavy: bfloat16 [2, 2048, 1024], P('doc', ('coarse', 'fine')), may hold values from -8 to 8
- k_heavy: bfloat16 [2, 2048, 1024], P('doc', ('coarse', 'fine')), may hold values from -8 to 8
- v_heavy: bfloat16 [2, 2048, 1024], P('doc', ('coarse', 'fine')), may hold values from -6 to 6
- enc_kv: bfloat16 [2, 2048, 128], P('doc', ('coarse', 'fine')), may hold values from -8 to 8
- dec_queries: bfloat16 [2, 512, 1024], P('doc'), may hold values from -8 to 8
- query_ids: int32 [2, 16], P('doc'), may hold values from 0 to 15, as said below
- key_ids: int32 [2, 16], P('doc'), may hold values from 0 to 15, as said below
Outputs:
- encoded: bfloat16 [2, 2048, 1024], P('doc', ('coarse', 'fine'))
- decoded: bfloat16 [2, 512, 1024], P('doc')
Inputs may be any that keep to these rules, and one draw needn't show every extreme that they name: `query_ids`: for each document and each c below the number of coarse groups, entries c * 8 to (c + 1) * 8 - 1 are distinct block numbers among blocks c * 8 to (c + 1) * 8 - 1 (so every block of the group is listed), and entry c * 8 + f is the block assigned to the f-th device of that group. `key_ids`: for each document and each c below the number of coarse groups, entries c * 8 to (c + 1) * 8 - 1 are distinct block numbers among blocks c * 8 * 1 to (c + 1) * 8 - 1.
All inputs are finite; a program needn't handle non-finite values.
Results may differ from a plain program's by a relative error of at most 0.009.
Values may be sent and summed in bfloat16 or wider, within the bound.
A program may use at most 384 MiB of HBM per device.

v0:
```python
import jax
import jax.numpy as jnp
from jax import lax
from jax.sharding import PartitionSpec as P

HEAD = 64
ROUTED_BLOCK = 128
KGRP = 8


def with_halo(block, sides, width):
    for axis, dim in sides:
        count = lax.axis_size(axis)
        forward = [(i, i + 1) for i in range(count - 1)]
        backward = [(target, source) for source, target in forward]
        low = lax.ppermute(
            lax.slice_in_dim(block, block.shape[dim] - width, None, axis=dim), axis, forward
        )
        high = lax.ppermute(lax.slice_in_dim(block, 0, width, axis=dim), axis, backward)
        block = jnp.concatenate([low, block, high], axis=dim)
    return block


def merged(value, axis, join):
    pieces = jax.tree.map(lambda part: lax.all_gather(part, axis), value)
    head = jax.tree.map(lambda part: part[0], pieces)
    tail = jax.tree.map(lambda part: part[1:], pieces)
    running, _ = lax.scan(lambda running, share: (join(running, share), None), head, tail)
    return running


def attend(query, keys, value_rows, mask):
    rows = query.shape[0]
    count = keys.shape[0]
    heads = query.shape[1] // HEAD
    qh = query.reshape(rows, heads, HEAD).transpose(1, 0, 2)
    kh = keys.reshape(count, heads, HEAD).transpose(1, 0, 2)
    vh = value_rows.reshape(count, heads, HEAD).transpose(1, 0, 2)

    def one_head(triple):
        qa, ka, va = triple
        scores = jnp.dot(qa, ka.T, preferred_element_type=jnp.float32) * HEAD ** (-0.5)
        if mask is not None:
            scores = jnp.where(mask, scores, jnp.float32(-1e30))
        peak = jnp.max(scores, axis=1, keepdims=True)
        weights = jnp.exp(scores - peak)
        weights = (weights / jnp.sum(weights, axis=1, keepdims=True)).astype(jnp.bfloat16)
        return jnp.dot(weights, va, preferred_element_type=jnp.float32)

    out = lax.map(one_head, (qh, kh, vh))
    return out.transpose(1, 0, 2).reshape(rows, heads * HEAD)


def combine(leading_entry, second):
    peak = jnp.maximum(leading_entry[0], second[0])
    scale_a = jnp.exp(leading_entry[0] - peak)
    scale_b = jnp.exp(second[0] - peak)
    total = leading_entry[1] * scale_a + second[1] * scale_b
    value_rows = leading_entry[2] * scale_a[..., None] + second[2] * scale_b[..., None]
    return (peak, total, value_rows)


def local(
    q_light, k_light, v_light, q_heavy, k_heavy, v_heavy, enc_kv, dec_queries, query_ids, key_ids
):
    query = q_light[0]
    tokens, width = query.shape
    n_seq = lax.axis_size(("coarse", "fine"))
    n_fine = lax.axis_size("fine")
    here = lax.axis_index(("coarse", "fine"))
    group = lax.axis_index("coarse")
    start = here * tokens
    light_kv = jnp.concatenate([k_light[0], v_light[0]], axis=1)
    padded = with_halo(light_kv, ((("coarse", "fine"), 0),), ROUTED_BLOCK)
    key_pos = start - ROUTED_BLOCK + jnp.arange(tokens + 2 * ROUTED_BLOCK, dtype=jnp.int32)
    inside = (key_pos >= 0) & (key_pos < tokens * n_seq)
    rows = min(512, tokens)
    qpos = start + 0 + jnp.arange(rows, dtype=jnp.int32)
    mask = (jnp.abs(qpos[:, None] - key_pos[None, :]) <= ROUTED_BLOCK - 1) & inside[None, :]
    pieces = attend(query, padded[:, :width], padded[:, width:], mask)
    blocks = tokens // ROUTED_BLOCK
    mine = here * blocks + jnp.arange(blocks, dtype=jnp.int32)
    key_group = lax.dynamic_slice_in_dim(key_ids[0], group * KGRP, KGRP)
    pick_keys = (key_group[:, None] == mine[None, :]).astype(jnp.bfloat16)
    heavy_kv = jnp.concatenate([k_heavy[0], v_heavy[0]], axis=1).reshape(
        blocks, ROUTED_BLOCK, 2 * width
    )
    slots = jnp.einsum(
        "sb,bre->sre", pick_keys, heavy_kv, preferred_element_type=jnp.float32
    ).reshape(KGRP * ROUTED_BLOCK, 2 * width)
    share = lax.psum_scatter(slots.astype(jnp.bfloat16), "fine", scatter_dimension=0, tiled=True)
    keys_all = lax.all_gather(share, ("coarse", "fine"), axis=0, tiled=True)
    query_group = lax.dynamic_slice_in_dim(query_ids[0], group * n_fine, n_fine)
    pick_rows = (query_group[:, None] == mine[None, :]).astype(jnp.bfloat16)
    heavy_query = q_heavy[0]
    result = attend(heavy_query, keys_all[:, :width], keys_all[:, width:], None).astype(
        jnp.bfloat16
    )
    chosen = jnp.sum(pick_rows.astype(jnp.float32), axis=0)
    heavy = (
        result.reshape(blocks, ROUTED_BLOCK, width).astype(jnp.float32) * chosen[:, None, None]
    ).reshape(tokens, width)
    encoded = (pieces + heavy).astype(jnp.bfloat16)[None]
    decoder_query_rows = dec_queries[0]
    count = decoder_query_rows.shape[0]
    heads = width // HEAD
    enc_keys = enc_kv[0][:, :HEAD]
    enc_values = enc_kv[0][:, HEAD:]
    heads_query = decoder_query_rows.reshape(count, heads, HEAD).transpose(1, 0, 2)

    def partial_head(qa):
        scores = jnp.dot(qa, enc_keys.T, preferred_element_type=jnp.float32) * HEAD ** (-0.5)
        peak = jnp.max(scores, axis=1)
        weights = jnp.exp(scores - peak[:, None])
        total = jnp.sum(weights, axis=1)
        value_rows = jnp.dot(
            weights.astype(jnp.bfloat16), enc_values, preferred_element_type=jnp.float32
        )
        return (peak, total, value_rows)

    peak, total, value_rows = lax.map(partial_head, heads_query)
    peak, total, value_rows = merged((peak, total, value_rows), ("coarse", "fine"), combine)
    decoded = (
        (value_rows / total[..., None])
        .transpose(1, 0, 2)
        .reshape(count, width)
        .astype(jnp.bfloat16)[None]
    )
    return (encoded, decoded)


def solution(mesh):
    placed = (
        P("doc", ("coarse", "fine"), None),
        P("doc", ("coarse", "fine"), None),
        P("doc", ("coarse", "fine"), None),
        P("doc", ("coarse", "fine"), None),
        P("doc", ("coarse", "fine"), None),
        P("doc", ("coarse", "fine"), None),
        P("doc", ("coarse", "fine"), None),
        P("doc", None, None),
        P("doc", None),
        P("doc", None),
    )
    return jax.shard_map(
        local,
        mesh=mesh,
        in_specs=placed,
        out_specs=(P("doc", ("coarse", "fine"), None), P("doc", None, None)),
        check_vma=False,
    )
```

profile of v0, /device:TPU:10, one launch (start us, length us, event | category | flops | bytes accessed | tf_op | source)
XLA Modules:
  0.0 875.9 jit_solution(11162290287777442142)
XLA Ops:
  9.4 2.4 multiply_convert_fusion
  11.8 6.7 copy.52
  18.5 89.7 %reduce-scatter.4.cloned.1.call-done = bf16[128,2048]{1,0:T(8,128)(2,1)} async-done(((bf16[1024,2048]{1,0:T(8,128)(2,1)}), bf16[128,2048]{1,0:T(8,128)(2,1)}) %reduce-scatter.4.cloned.1.call-update) | async-done | bytes 524304
  108.3 2.1 copy.51
  111.1 20.2 %while.54 = (s32[]{:T(128)}, f32[16,512]{1,0:T(8,128)S(1)}, f32[16,512]{1,0:T(8,128)S(1)}, f32[16,512,64]{1,2,0:T(8,128)}, bf16[16,512,64]{1,2,0:T(8,128)(2,1)S(...) while((s32[]{:T(128)}, f32[16,512]{1,0:T(8,128)S(1)}, ...), condition=%wide.region_13.14_spmd.clone, body=%wide.region_10.13_spmd.sunk.clone | while | flops 17169408 | bytes 1049177 | solution.py:121
  131.8 3.4 collective-permute-start
  135.2 3.3 collective-permute-start.1
  138.6 68.6 %all-gather = f32[256,512]{1,0:T(8,128)S(1)} all-gather(f32[16,512]{1,0:T(8,128)S(1)} %get-tuple-element.140), channel_id=2, replica_groups=mesh['doc'=2,'coarse'=2,'fine'=8] {'coarse','fine'}, dimensions={0}, use_global_device_ids=true | all-gather | bytes 557056 | tf_op jit(solution)/shard_map/all_gather | solution.py:25
  207.2 47.6 %all-gather.1 = f32[256,512]{1,0:T(8,128)S(1)} all-gather(f32[16,512]{1,0:T(8,128)S(1)} %get-tuple-element.141), channel_id=3, replica_groups=mesh['doc'=2,'coarse'=2,'fine'=8] {'coarse','fine'}, dimensions={0}, use_global_device_ids=true | all-gather | bytes 557056 | tf_op jit(solution)/shard_map/all_gather | solution.py:25
  261.8 25.5 %while.56 = (s32[]{:T(128)}, f32[16,128,64]{1,2,0:T(8,128)S(1)}, bf16[16,128,64]{1,2,0:T(8,128)(2,1)}, bf16[16,384,64]{1,2,0:T(8,128)(2,1)}, bf16[16,384,64]{1,2...) while((s32[]{:T(128)}, f32[16,128,64]{1,2,0:T(8,128)S(1)}, ...), condition=%wide.region_3.4_spmd.clone.clone, body=%wide.region_0.3_spmd.clone.sunk.clone | while | flops 13172482 | bytes 744405 | solution.py:50
  287.3 6.0 fusion.44
  293.3 48.5 %while.53 = (s32[]{:T(128)}, bf16[16,128,64]{1,2,0:T(8,128)(2,1)S(1)}, bf16[16,128,64]{1,2,0:T(8,128)(2,1)S(1)}, bf16[16,2048,64]{1,2,0:T(8,128)(2,1)}, bf16[16,2048,64]{1,2,0:T(8,128)(2,1)}) while((s32[]{:T(128)}, bf16[16,128,64]{1,2,0:T(8,128)(2,1)S(1)}, bf16[16,128,64]{1,2,0:T(8,128)(2,1)S(1)}, bf16[16,2048,64]{1,2,0:T(8,128)(2,1)}, ...), condition=%wide.region_8.9_spmd.clone, body=%wide.region_5.8_spmd.sunk.clone | while | flops 68943616 | bytes 3723837 | solution.py:50
  343.5 294.3 %all-gather.8.cloned.1.call-done = f32[256,512,64]{1,2,0:T(8,128)} async-done(((f32[16,512,64]{1,2,0:T(8,128)}), f32[256,512,64]{1,2,0:T(8,128)}) %all-gather.8.cloned.1.call-update) | async-done | bytes 33554448 | tf_op jit(solution)/shard_map/all_gather | solution.py:25
  639.4 2.7 copy.45
  642.1 22.9 %slice.65 = f32[240,512,64]{1,2,0:T(8,128)} slice(f32[256,512,64]{1,2,0:T(8,128)} %all-gather.8.cloned.1.call-done), slice={[16:256], [0:512], [0:64]} | slice | bytes 62914560 | tf_op jit(solution)/shard_map/slice | solution.py:27
  665.0 199.9 %while.55 = (s32[]{:T(128)}, f32[16,512]{1,0:T(8,128)S(1)}, f32[16,512]{1,0:T(8,128)S(1)}, f32[16,512,64]{2,1,0:T(8,128)}, f32[15,16,512]{2,1,0:T(8,128)}, /*ind...) while((s32[]{:T(128)}, f32[16,512]{1,0:T(8,128)S(1)}, f32[16,512]{1,0:T(8,128)S(1)}, ...), condition=%wide.region_15.16_spmd.clone, body=%wide.region_14.15_spmd.sunk.clone | while | flops 1622018 | bytes 15007829 | solution.py:28
  665.8 1.9 constant_dynamic-slice_fusion.3
  667.6 2.7 copy.63
  670.4 7.9 fusion.92
  681.0 2.7 copy.63
  683.7 7.9 fusion.92
  694.3 2.7 copy.63
  697.0 7.9 fusion.92
  707.6 2.7 copy.63
  710.3 7.9 fusion.92
  720.9 2.7 copy.63
  723.7 7.9 fusion.92
  734.3 2.7 copy.63
  737.0 7.9 fusion.92
  747.6 2.7 copy.63
  750.3 7.9 fusion.92
  760.9 2.7 copy.63
  763.7 7.9 fusion.92
  774.3 2.7 copy.63
  777.0 7.9 fusion.92
  787.6 2.7 copy.63
  790.3 7.9 fusion.92
  800.9 2.7 copy.63
  803.6 7.9 fusion.92
  814.3 2.7 copy.63
  817.0 7.9 fusion.92
  827.6 2.7 copy.63
  830.3 7.9 fusion.92
  840.9 2.7 copy.63
  843.6 7.9 fusion.92
  854.2 2.7 copy.63
  857.0 7.9 fusion.92
  864.9 2.8 copy.47
  (263 shorter events, 146.2 us)
Async XLA Ops:
  7.2 101.1 %reduce-scatter.4.cloned.1.call-start = ((), (), s32[]{:S(2)}) async-start(), calls=%async_computation.3 | async-start | bytes 4718592
  18.5 92.0 %copy-start.2 = (bf16[1,512,1024]{2,1,0:T(8,128)(2,1)S(1)}, bf16[1,512,1024]{2,1,0:T(8,128)(2,1)}, u32[]{:S(2)}) copy-start(bf16[1,512,1024]{2,1,0:T(8,128)(2,1)} %param.25) | copy-start | bytes 3145732
  18.5 92.6 %copy-start.6 = (bf16[1,128,128]{2,1,0:T(8,128)(2,1)S(1)}, bf16[1,128,128]{2,1,0:T(8,128)(2,1)}, u32[]{:S(2)}) copy-start(bf16[1,128,128]{2,1,0:T(8,128)(2,1)} %param.24) | copy-start | bytes 98308
  18.5 268.8 %all-gather.6.cloned.1.call-start = ((), (), s32[]{:S(2)}) async-start(), calls=%async_computation.1 | async-start | bytes 8912896 | tf_op jit(solution)/shard_map/all_gather | solution.py:92
  110.4 527.4 %all-gather.8.cloned.1.call-start = ((), (), s32[]{:S(2)}) async-start(), calls=%async_computation.2 | async-start | bytes 35651584 | tf_op jit(solution)/shard_map/all_gather | solution.py:25
  111.0 20.4 %copy-start.3 = (bf16[1,128,1024]{2,1,0:T(8,128)(2,1)S(1)}, bf16[1,128,1024]{2,1,0:T(8,128)(2,1)}, u32[]{:S(2)}) copy-start(bf16[1,128,1024]{2,1,0:T(8,128)(2,1)} %param.19) | copy-start | bytes 786436
  111.0 20.6 %copy-start.4 = (bf16[1,128,1024]{2,1,0:T(8,128)(2,1)S(1)}, bf16[1,128,1024]{2,1,0:T(8,128)(2,1)}, u32[]{:S(2)}) copy-start(bf16[1,128,1024]{2,1,0:T(8,128)(2,1)} %param.20) | copy-start | bytes 786436
  131.4 125.1 %copy-start.5 = (bf16[1,128,1024]{2,1,0:T(8,128)(2,1)S(1)}, bf16[1,128,1024]{2,1,0:T(8,128)(2,1)}, u32[]{:S(2)}) copy-start(bf16[1,128,1024]{2,1,0:T(8,128)(2,1)} %param.18) | copy-start | bytes 786436
  131.4 127.1 %copy-start.7 = (s32[1,16]{1,0:T(1,128)S(1)}, s32[1,16]{1,0:T(1,128)}, u32[]{:S(2)}) copy-start(s32[1,16]{1,0:T(1,128)} %param.26) | copy-start | bytes 196
  131.8 127.4 %collective-permute-start = (bf16[128,2048]{0,1:T(8,128)(2,1)S(1)}, bf16[128,2048]{0,1:T(8,128)(2,1)}, u32[]{:S(2)}, u32[]{:S(2)}) collective-permute-start(bf16[128,2048]{0,1:T(8,128)(2,1)S(1)} %pad_maximum_fusion.1), channel_id=1, source_target_pairs={{0,1},{1,2},{2,3},{3,4},{4,5},{5,6},{6,7},{7,8},{8,9},{9,10},{10,1... | collective-permute-start | bytes 1572872 | tf_op jit(solution)/shard_map/ppermute | solution.py:16
  135.2 124.0 %collective-permute-start.1 = (bf16[128,2048]{0,1:T(8,128)(2,1)S(1)}, bf16[128,2048]{0,1:T(8,128)(2,1)}, u32[]{:S(2)}, u32[]{:S(2)}) collective-permute-start(bf16[128,2048]{0,1:T(8,128)(2,1)S(1)} %pad_maximum_fusion.1), channel_id=1, source_target_pairs={{1,0},{2,1},{3,2},{4,3},{5,4},{6,5},{7,6},{8,7},{9,8},{10,9},{11,1... | collective-permute-start | bytes 1572872 | tf_op jit(solution)/shard_map/ppermute | solution.py:19
  207.2 86.2 %copy-start = (f32[256,512]{1,0:T(8,128)}, f32[256,512]{1,0:T(8,128)S(1)}, u32[]{:S(2)}) copy-start(f32[256,512]{1,0:T(8,128)S(1)} %all-gather) | copy-start | bytes 1572868
  254.8 38.6 %copy-start.1 = (f32[256,512]{1,0:T(8,128)}, f32[256,512]{1,0:T(8,128)S(1)}, u32[]{:S(2)}) copy-start(f32[256,512]{1,0:T(8,128)S(1)} %all-gather.1) | copy-start | bytes 1572868
  637.8 1.6 slice-start
  642.1 22.9 %slice-start.1 = ((f32[256,512]{1,0:T(8,128)}), f32[16,512]{1,0:T(8,128)S(1)}, s32[]{:S(2)}) async-start(f32[256,512]{1,0:T(8,128)} %copy-done), calls=%async_computation.5 | async-start | bytes 65536 | tf_op jit(solution)/shard_map/slice | solution.py:26
  642.1 22.9 %slice-start.2 = ((f32[256,512]{1,0:T(8,128)}), f32[16,512]{1,0:T(8,128)S(1)}, s32[]{:S(2)}) async-start(f32[256,512]{1,0:T(8,128)} %copy-done.1), calls=%async_computation.6 | async-start | bytes 65536 | tf_op jit(solution)/shard_map/slice | solution.py:26
Sparse Core Ops, SparseCore 0:
  18.6 89.6 reduce-scatter.3
  111.0 173.0 all-gather.5
  286.8 350.8 all-gather.7
where the time goes:
time: 885 us; the launch traced here: 876 us
  waiting for transfers between devices  384 us (43%)
  other arithmetic  148 us (17%)
  local copies, waits for them, and re-layouts  123 us (14%)
  blocking collectives  116 us (13%)
  matrix products  82.1 us (9%)
  between operations  14 us (2%)
    all_gather x1, waiting for transfers between devices, merged(): pieces = jax.tree.map(lambda part: lax.all_gather(part, axis), value)  294 us
    add x15, other arithmetic, combine(): leading_entry[2] * scale_a[..., None] + second[2] * scale_b[..., None]  119 us
    all_gather x2, blocking collectives, merged(): pieces = jax.tree.map(lambda part: lax.all_gather(part, axis), value)  116 us
    unnamed x4, waiting for transfers between devices  89.8 us
    dynamic_slice x30, local copies, waits for them, and re-layouts, merged(): lax.scan(lambda running, share: (join(running, share), None), head, tail)  68.7 us
    dot_general x32, matrix products, one_head(): jnp.dot(qa, ka.T, preferred_element_type=jnp.float32) * HEAD ** (-0.5)  39.7 us
    dot_general x32, matrix products, one_head(): return jnp.dot(weights, va, preferred_element_type=jnp.float32)  25.6 us
    slice x3, local copies, waits for them, and re-layouts, merged(): tail = jax.tree.map(lambda part: part[1:], pieces)  24.6 us
  transfers between devices with their start and end apart: 5, of which 2 were waited for; matrix products, arithmetic and copies ran while one was open for 12% of the time, Pallas kernels for 0%

commit v1 on v0

v1 whole, which is shorter than its diff:
```python
import functools

import jax
import jax.numpy as jnp
from jax import lax
from jax.experimental import pallas as pl
from jax.experimental.pallas import tpu as pltpu
from jax.sharding import PartitionSpec as P

HEAD = 64
PAIR = 2 * HEAD
ROUTED_BLOCK = 128
KGRP = 8
LOW = 2
MESH = pl.DeviceIdType.MESH
NEG = -1e30


def dot_t(a, b):
    return lax.dot_general(a, b, (((1,), (1,)), ((), ())), preferred_element_type=jnp.float32)


def dot(a, b):
    return jnp.dot(a, b, preferred_element_type=jnp.float32)


def stacked_pair(q, low_half):
    q = q * jnp.asarray(HEAD ** (-0.5), q.dtype)
    zero = jnp.zeros_like(q)
    return jnp.concatenate([jnp.where(low_half, q, zero), jnp.where(low_half, zero, q)], axis=0)


def kernel(dims, has_bias, *refs):
    n_coarse, n_fine, tokens, width, dec_rows = dims
    n_seq = n_coarse * n_fine
    n_q = n_fine // LOW
    n_kv = n_coarse * LOW
    heads = width // HEAD
    pairs = heads // 2
    refs = list(refs)
    ql, kl, vl, qh, kh, vh, enc, decq = refs[:8]
    bias_ref = refs[8] if has_bias else None
    (out, dec, encbuf, dq, do, qbuf, kbuf, vbuf, khalo, vhalo, osend, orecv, ssend, srecv,
     wts, light, band, enc_s, enc_r, dec_s, dec_r, q_s, q_r, k_s, k_r, v_s, v_r,
     o_s, o_r, st_s, st_r, h_s, h_r) = refs[8 + has_bias:]

    c = lax.axis_index("coarse")
    f = lax.axis_index("fine")
    here = c * n_fine + f
    me_q = lax.div(f, LOW)
    lo = lax.rem(f, LOW)
    me_kv = c * LOW + lo

    def at_seq(s):
        return {"coarse": lax.div(s, n_fine), "fine": lax.rem(s, n_fine)}

    def at_q(a):
        return {"coarse": c, "fine": a * LOW + lo}

    def at_kv(b):
        return {"coarse": lax.div(b, LOW), "fine": me_q * LOW + lax.rem(b, LOW)}

    def remote(src, dst, ssem, rsem, device):
        return pltpu.make_async_remote_copy(
            src_ref=src, dst_ref=dst, send_sem=ssem, recv_sem=rsem,
            device_id=device, device_id_type=MESH,
        )

    def up(me, d, n):
        return lax.rem(me + d, n)

    def down(me, d, n):
        return lax.rem(me + n - d, n)

    barrier = pltpu.get_barrier_semaphore()

    def greet(d, carry):
        pl.semaphore_signal(barrier, inc=1, device_id=at_seq(up(here, d, n_seq)), device_id_type=MESH)
        return carry

    lax.fori_loop(1, n_seq, greet, 0)
    pl.semaphore_wait(barrier, n_seq - 1)

    def enc_copy(d):
        peer = up(here, d, n_seq)
        return remote(enc, encbuf.at[here], enc_s.at[d], enc_r.at[here], at_seq(peer))

    def enc_arrival(d):
        src = down(here, d, n_seq)
        return remote(enc, encbuf.at[src], enc_s.at[d], enc_r.at[src], at_seq(src))

    def q_copy(d):
        return remote(qh, qbuf.at[me_q], q_s.at[d], q_r.at[me_q], at_q(up(me_q, d, n_q)))

    def q_arrival(d):
        src = up(me_q, d, n_q)
        return remote(qh, qbuf.at[src], q_s.at[d], q_r.at[src], at_q(src))

    def kv_copy(ref, buf, ss, rs, d):
        return remote(ref, buf.at[me_kv], ss.at[d], rs.at[me_kv], at_kv(up(me_kv, d, n_kv)))

    def kv_arrival(ref, buf, ss, rs, d):
        src = down(me_kv, d, n_kv)
        return remote(ref, buf.at[src], ss.at[d], rs.at[src], at_kv(src))

    def o_copy(d):
        peer = up(me_q, d, n_q)
        return (
            remote(osend.at[peer], orecv.at[me_q], o_s.at[d], o_r.at[me_q], at_q(peer)),
            remote(ssend.at[peer], srecv.at[me_q], st_s.at[d], st_r.at[me_q], at_q(peer)),
        )

    def o_arrival(d):
        src = down(me_q, d, n_q)
        return (
            remote(osend.at[src], orecv.at[src], o_s.at[d], o_r.at[src], at_q(src)),
            remote(ssend.at[src], srecv.at[src], st_s.at[d], st_r.at[src], at_q(src)),
        )

    def dec_copy(d):
        peer = up(here, d, n_seq)
        return remote(dec.at[here], dec.at[here], dec_s.at[d], dec_r.at[here], at_seq(peer))

    def dec_arrival(d):
        src = down(here, d, n_seq)
        return remote(dec.at[src], dec.at[src], dec_s.at[d], dec_r.at[src], at_seq(src))

    def halo_copy(side):
        peer = jnp.clip(here + 1 - 2 * side, 0, n_seq - 1)
        return (
            remote(kl, khalo.at[side], h_s.at[side, 0], h_r.at[side, 0], at_seq(peer)),
            remote(vl, vhalo.at[side], h_s.at[side, 1], h_r.at[side, 1], at_seq(peer)),
        )

    def loop(start, stop, body):
        def step(d, carry):
            body(d)
            return carry
        lax.fori_loop(start, stop, step, 0)

    loop(1, n_seq, lambda d: enc_copy(d).start())
    for d in range(1, n_q):
        q_copy(d).start()
    for d in range(1, n_kv):
        kv_copy(kh, kbuf, k_s, k_r, d).start()
        kv_copy(vh, vbuf, v_s, v_r, d).start()
    has_next = here < n_seq - 1
    has_prev = here > 0

    @pl.when(has_next)
    def _():
        for copy in halo_copy(0):
            copy.start()

    @pl.when(has_prev)
    def _():
        for copy in halo_copy(1):
            copy.start()

    encbuf[here] = enc[...]
    qbuf[me_q] = qh[...]
    kbuf[me_kv] = kh[...]
    vbuf[me_kv] = vh[...]
    row = lax.broadcasted_iota(jnp.int32, (tokens, 3 * tokens), 0)
    col = lax.broadcasted_iota(jnp.int32, (tokens, 3 * tokens), 1)
    pos = here * tokens + col - tokens
    seen = (jnp.abs(col - tokens - row) <= ROUTED_BLOCK - 1) & (pos >= 0) & (pos < n_seq * tokens)
    band[...] = jnp.where(seen, jnp.float32(0), jnp.float32(NEG))

    lane_d = lax.broadcasted_iota(jnp.int32, (dec_rows, PAIR), 1)
    for j in range(pairs):
        q = decq[0, :, j * PAIR:(j + 1) * PAIR].astype(jnp.float32) * (HEAD ** (-0.5))
        swapped = pltpu.roll(q, HEAD, 1)
        both = jnp.concatenate(
            [jnp.where(lane_d < HEAD, q, 0.0), jnp.where(lane_d < HEAD, swapped, 0.0)], axis=0
        )
        dq[2 * j * dec_rows:(2 * j + 2) * dec_rows, :] = both.astype(jnp.bfloat16)
    loop(1, n_seq, lambda d: enc_arrival(d).wait_recv())
    d_total = heads * dec_rows
    d_chunk = min(256, d_total)

    def dec_step(i):
        rows = pl.ds(pl.multiple_of(i * d_chunk, d_chunk), d_chunk)
        kv = encbuf[...].reshape(n_seq * tokens, PAIR)
        s = dot_t(dq[rows, :], kv)
        p = jnp.exp(s - jnp.max(s, axis=1, keepdims=True))
        total = jnp.sum(p, axis=1, keepdims=True)
        do[rows, :] = dot(p.astype(jnp.bfloat16), kv) / total

    loop(0, d_total // d_chunk, dec_step)
    for j in range(pairs):
        even = do[2 * j * dec_rows:(2 * j + 1) * dec_rows, :]
        odd = do[(2 * j + 1) * dec_rows:(2 * j + 2) * dec_rows, :]
        dec[here, :, j * PAIR:(j + 1) * PAIR] = jnp.where(
            lane_d < HEAD, pltpu.roll(even, HEAD, 1), odd
        ).astype(jnp.bfloat16)
    loop(1, n_seq, lambda d: dec_copy(d).start())

    low_half = lax.broadcasted_iota(jnp.int32, (tokens, PAIR), 1) < HEAD
    lane = lax.broadcasted_iota(jnp.int32, (tokens, PAIR), 1)
    for d in range(1, n_kv):
        kv_arrival(kh, kbuf, k_s, k_r, d).wait_recv()
        kv_arrival(vh, vbuf, v_s, v_r, d).wait_recv()
    for d in list(range(1, n_q)) + [0]:
        block = up(me_q, d, n_q)
        if d:
            q_arrival(d).wait_recv()

        def pair_step(j, stat):
            cols = pl.ds(pl.multiple_of(j * PAIR, PAIR), PAIR)
            q = stacked_pair(qbuf[block, :, cols], low_half)
            s = dot_t(q, kbuf[:, :, cols].reshape(n_kv * tokens, PAIR))
            if has_bias:
                s = s + bias_ref[0:1, :]
            peak = jnp.max(s, axis=1, keepdims=True)
            p = jnp.exp(s - peak)
            total = jnp.sum(p, axis=1, keepdims=True)
            o = dot(p.astype(jnp.bfloat16), vbuf[:, :, cols].reshape(n_kv * tokens, PAIR)) / total
            lse = peak + jnp.log(total)
            osend[block, :, cols] = jnp.where(low_half, o[:tokens], o[tokens:]).astype(jnp.bfloat16)
            stat = jnp.where(lane == 2 * j, lse[:tokens], stat)
            return jnp.where(lane == 2 * j + 1, lse[tokens:], stat)

        stat = lax.fori_loop(0, pairs, pair_step, jnp.zeros((tokens, PAIR), jnp.float32))
        ssend[block] = stat.T[:heads]
        if d:
            for copy in o_copy(d):
                copy.start()
        else:
            wts[0] = stat

    @pl.when(has_prev)
    def _():
        for copy in halo_copy(0):
            copy.wait_recv()

    @pl.when(jnp.logical_not(has_prev))
    def _():
        khalo[0] = jnp.zeros_like(kl)
        vhalo[0] = jnp.zeros_like(vl)

    @pl.when(has_next)
    def _():
        for copy in halo_copy(1):
            copy.wait_recv()

    @pl.when(jnp.logical_not(has_next))
    def _():
        khalo[1] = jnp.zeros_like(kl)
        vhalo[1] = jnp.zeros_like(vl)

    def light_step(j):
        cols = pl.ds(pl.multiple_of(j * PAIR, PAIR), PAIR)
        q = stacked_pair(ql[:, cols], low_half)
        keys = jnp.concatenate([khalo[0, :, cols], kl[:, cols], khalo[1, :, cols]], axis=0)
        rows = jnp.concatenate([vhalo[0, :, cols], vl[:, cols], vhalo[1, :, cols]], axis=0)
        mask = band[...]
        s = dot_t(q, keys) + jnp.concatenate([mask, mask], axis=0)
        p = jnp.exp(s - jnp.max(s, axis=1, keepdims=True))
        total = jnp.sum(p, axis=1, keepdims=True)
        o = dot(p.astype(jnp.bfloat16), rows) / total
        light[:, cols] = jnp.where(low_half, o[:tokens], o[tokens:])

    loop(0, pairs, light_step)

    for d in range(1, n_q):
        for copy in o_arrival(d):
            copy.wait_recv()
        pad = jnp.zeros((PAIR - heads, tokens), jnp.float32)
        wts[d] = jnp.concatenate([srecv[down(me_q, d, n_q)], pad], axis=0).T
    top = wts[0]
    for d in range(1, n_q):
        top = jnp.maximum(top, wts[d])
    norm = jnp.zeros_like(top)
    for d in range(n_q):
        share = jnp.exp(wts[d] - top)
        wts[d] = share
        norm = norm + share
    for d in range(n_q):
        wts[d] = wts[d] / norm

    def join_step(j):
        cols = pl.ds(pl.multiple_of(j * PAIR, PAIR), PAIR)
        acc = jnp.zeros((tokens, PAIR), jnp.float32)
        for d in range(n_q):
            part = osend[me_q, :, cols] if d == 0 else orecv[down(me_q, d, n_q), :, cols]
            w = wts[d]
            even = jnp.sum(jnp.where(lane == 2 * j, w, 0.0), axis=1, keepdims=True)
            odd = jnp.sum(jnp.where(lane == 2 * j + 1, w, 0.0), axis=1, keepdims=True)
            acc = acc + jnp.where(low_half, even, odd) * part.astype(jnp.float32)
        heavy = acc.astype(jnp.bfloat16).astype(jnp.float32)
        out[:, cols] = (light[:, cols] + heavy).astype(jnp.bfloat16)

    loop(0, pairs, join_step)

    loop(1, n_seq, lambda d: dec_arrival(d).wait_recv())
    loop(1, n_seq, lambda d: enc_copy(d).wait_send())
    loop(1, n_seq, lambda d: dec_copy(d).wait_send())
    for d in range(1, n_q):
        q_copy(d).wait_send()
        for copy in o_copy(d):
            copy.wait_send()
    for d in range(1, n_kv):
        kv_copy(kh, kbuf, k_s, k_r, d).wait_send()
        kv_copy(vh, vbuf, v_s, v_r, d).wait_send()

    @pl.when(has_next)
    def _():
        for copy in halo_copy(0):
            copy.wait_send()

    @pl.when(has_prev)
    def _():
        for copy in halo_copy(1):
            copy.wait_send()


def local(
    q_light, k_light, v_light, q_heavy, k_heavy, v_heavy, enc_kv, dec_queries, query_ids, key_ids
):
    _, tokens, width = q_light.shape
    n_coarse = lax.axis_size("coarse")
    n_fine = lax.axis_size("fine")
    n_seq = n_coarse * n_fine
    n_q = n_fine // LOW
    n_kv = n_coarse * LOW
    heads = width // HEAD
    count = dec_queries.shape[1]
    dec_rows = count // n_seq
    here = lax.axis_index(("coarse", "fine"))
    mine = lax.dynamic_slice_in_dim(dec_queries.reshape(n_seq, dec_rows, width), here, 1)
    args = [q_light[0], k_light[0], v_light[0], q_heavy[0], k_heavy[0], v_heavy[0], enc_kv[0], mine]
    has_bias = key_ids.shape[1] != n_seq
    if has_bias:
        high = lax.div(lax.axis_index("fine"), LOW)
        member = jnp.arange(n_kv, dtype=jnp.int32)
        blocks = (member // LOW) * n_fine + high * LOW + member % LOW
        listed = jnp.any(blocks[:, None] == key_ids[0][None, :], axis=1)
        bias = jnp.repeat(jnp.where(listed, 0.0, NEG).astype(jnp.float32), tokens)
        args.append(jnp.broadcast_to(bias[None], (8, n_kv * tokens)))
    bf16, f32 = jnp.bfloat16, jnp.float32
    dma = pltpu.SemaphoreType.DMA
    vmem = pl.BlockSpec(memory_space=pltpu.VMEM)
    encoded, decoded = pl.pallas_call(
        functools.partial(kernel, (n_coarse, n_fine, tokens, width, dec_rows), has_bias),
        out_shape=(
            jax.ShapeDtypeStruct((tokens, width), bf16),
            jax.ShapeDtypeStruct((n_seq, dec_rows, width), bf16),
        ),
        in_specs=[vmem] * len(args),
        out_specs=(vmem, vmem),
        scratch_shapes=[
            pltpu.VMEM((n_seq, tokens, PAIR), bf16),
            pltpu.VMEM((heads * dec_rows, PAIR), bf16),
            pltpu.VMEM((heads * dec_rows, PAIR), f32),
            pltpu.VMEM((n_q, tokens, width), bf16),
            pltpu.VMEM((n_kv, tokens, width), bf16),
            pltpu.VMEM((n_kv, tokens, width), bf16),
            pltpu.VMEM((2, tokens, width), bf16),
            pltpu.VMEM((2, tokens, width), bf16),
            pltpu.VMEM((n_q, tokens, width), bf16),
            pltpu.VMEM((n_q, tokens, width), bf16),
            pltpu.VMEM((n_q, heads, tokens), f32),
            pltpu.VMEM((n_q, heads, tokens), f32),
            pltpu.VMEM((n_q, tokens, PAIR), f32),
            pltpu.VMEM((tokens, width), f32),
            pltpu.VMEM((tokens, 3 * tokens), f32),
            dma((n_seq,)), dma((n_seq,)),
            dma((n_seq,)), dma((n_seq,)),
            dma((n_q,)), dma((n_q,)),
            dma((n_kv,)), dma((n_kv,)),
            dma((n_kv,)), dma((n_kv,)),
            dma((n_q,)), dma((n_q,)),
            dma((n_q,)), dma((n_q,)),
            dma((2, 2)), dma((2, 2)),
        ],
        compiler_params=pltpu.CompilerParams(
            collective_id=0, has_side_effects=True, vmem_limit_bytes=60 * 1024 * 1024
        ),
    )(*args)
    return encoded[None], decoded.reshape(1, count, width)


def solution(mesh):
    rows = P("doc", ("coarse", "fine"), None)
    placed = (rows,) * 7 + (P("doc", None, None), P("doc", None), P("doc", None))
    return jax.shard_map(
        local,
        mesh=mesh,
        in_specs=placed,
        out_specs=(rows, P("doc", None, None)),
        check_vma=False,
    )
```

time: 885 us -> 111 us (0.13)
  waiting for transfers between devices: 384 us -> 0 us
  other arithmetic: 148 us -> 0 us
  local copies, waits for them, and re-layouts: 123 us -> 5.78 us
  blocking collectives: 116 us -> 0 us
  Pallas kernels: 0 us -> 102 us
  matrix products: 82.1 us -> 0 us
  between operations: 14 us -> 0.65 us
    all_gather x2 -> x0, waiting for transfers between devices: 294 us -> none  [the longest x1 294 us: merged(): pieces = jax.tree.map(lambda part: lax.all_gather(part, axis), value)]
    add x32 -> x0, other arithmetic: 131 us -> none  [the longest x15 119 us: combine(): leading_entry[2] * scale_a[..., None] + second[2] * scale_b[..., None]]
    all_gather x2 -> x0, blocking collectives: 116 us -> none  [merged(): pieces = jax.tree.map(lambda part: lax.all_gather(part, axis), value)]
    pallas_call x0 -> x1, Pallas kernels: none -> 102 us  [local(): pl.pallas_call(functools.partial(kernel, (n_coarse, n_fine, tokens, width...]
    unnamed x4 -> x0, waiting for transfers between devices: 89.8 us -> none
    dot_general x96 -> x0, matrix products: 82.1 us -> none  [the longest x32 39.7 us: one_head(): jnp.dot(qa, ka.T, preferred_element_type=jnp.float32) * HEAD ** (-0.5)]
    dynamic_slice x30 -> x1, local copies, waits for them, and re-layouts: 68.7 us -> 0.63 us  [local(): lax.dynamic_slice_in_dim(dec_queries.reshape(n_seq, dec_rows, width), her...]
    slice x12 -> x0, local copies, waits for them, and re-layouts: 33.3 us -> none  [the longest x3 24.6 us: merged(): tail = jax.tree.map(lambda part: part[1:], pieces)]
  transfers between devices with their start and end apart: 5 -> 0, of which waited for: 2 -> 0; matrix products, arithmetic and copies ran while one was open for 12% -> 0% of each run, Pallas kernels for 0% -> 0%
where the time goes in v1:
time: 111 us; the launch traced here: 109 us
  Pallas kernels  102 us (92%)
  local copies, waits for them, and re-layouts  5.78 us (5%)
    pallas_call x1, Pallas kernels, local(): pl.pallas_call(functools.partial(kernel, (n_coarse, n_fine, tokens, width...  102 us
    unnamed x4, local copies, waits for them, and re-layouts  5.15 us

profile of v1, /device:TPU:10, one launch (start us, length us, event | category | flops | bytes accessed | tf_op | source)
XLA Modules:
  0.0 108.8 jit_solution(8281399545638728216)
XLA Ops:
  0.6 0.0 copy-start
  0.7 1.2 %copy-done = bf16[1,512,1024]{2,1,0:T(8,128)(2,1)S(1)} copy-done((bf16[1,512,1024]{2,1,0:T(8,128)(2,1)S(1)}, bf16[1,512,1024]{2,1,0:T(8,128)(2,1)}, u32[]{:S(2)}) %copy-start) | copy-done | bytes 1048600
  1.9 0.6 constant_dynamic-slice_fusion.refs_7_
  2.5 102.4 %shard_map.95 = (bf16[128,1024]{1,0:T(8,128)(2,1)}, bf16[16,32,1024]{2,1,0:T(8,128)(2,1)}) custom-call(bf16[128,1024]{1,0:T(8,128)(2,1)} %bitcast.12, bf16[128,1024]{1,0:T(8,128)(2,1)} %bitcast.13, bf16[128,1024]{1,0:T(8,128)(2,1)} %bitcast.14, bf16[128,1024]{1,0:T(8,128)(2,1)} %bitcast.15, bf16[128,1024]{1,0:T(8,128)(2,1)} %bitcast.16, ...), custom_call_target="tpu_custom_call" | custom-call | tf_op jit(solution)/shard_map/pallas_call | solution.py:344
  104.9 1.7 %copy.12 = bf16[1,128,1024]{2,1,0:T(8,128)(2,1)} copy(bf16[1,128,1024]{2,1,0:T(8,128)(2,1)} %bitcast.18) | data formatting | bytes 524288
  106.6 2.3 %copy.13 = bf16[1,512,1024]{2,1,0:T(8,128)(2,1)} copy(bf16[1,512,1024]{2,1,0:T(8,128)(2,1)} %bitcast.11) | data formatting | bytes 2097152
Async XLA Ops:
  0.6 1.2 %copy-start = (bf16[1,512,1024]{2,1,0:T(8,128)(2,1)S(1)}, bf16[1,512,1024]{2,1,0:T(8,128)(2,1)}, u32[]{:S(2)}) copy-start(bf16[1,512,1024]{2,1,0:T(8,128)(2,1)} %param.17) | copy-start | bytes 3145732

commit v2 on v1

--- a/solution.py
+++ b/solution.py
@@ -41,8 +41,8 @@
     ql, kl, vl, qh, kh, vh, enc, decq = refs[:8]
     bias_ref = refs[8] if has_bias else None
     (out, dec, encbuf, dq, do, qbuf, kbuf, vbuf, khalo, vhalo, osend, orecv, ssend, srecv,
-     wts, light, band, enc_s, enc_r, dec_s, dec_r, q_s, q_r, k_s, k_r, v_s, v_r,
-     o_s, o_r, st_s, st_r, h_s, h_r) = refs[8 + has_bias:]
+     wts, light, band, enc_s, enc_r, dec_s, dec_r, q_s, q_r, o_s, o_r, st_s, st_r, h_s, h_r,
+     ek_s, ek_r, dk_s, dk_r, k_s, k_r, v_s, v_r) = refs[8 + has_bias:]
 
     c = lax.axis_index("coarse")
     f = lax.axis_index("fine")
@@ -82,26 +82,86 @@
     pl.semaphore_wait(barrier, n_seq - 1)
 
     def enc_copy(d):
-        peer = up(here, d, n_seq)
-        return remote(enc, encbuf.at[here], enc_s.at[d], enc_r.at[here], at_seq(peer))
+        mine = encbuf.at[me_kv, me_q]
+        return remote(enc, mine, enc_s.at[d], enc_r.at[me_q], at_q(up(me_q, d, n_q)))
 
     def enc_arrival(d):
-        src = down(here, d, n_seq)
-        return remote(enc, encbuf.at[src], enc_s.at[d], enc_r.at[src], at_seq(src))
-
-    def q_copy(d):
-        return remote(qh, qbuf.at[me_q], q_s.at[d], q_r.at[me_q], at_q(up(me_q, d, n_q)))
-
-    def q_arrival(d):
-        src = up(me_q, d, n_q)
-        return remote(qh, qbuf.at[src], q_s.at[d], q_r.at[src], at_q(src))
-
-    def kv_copy(ref, buf, ss, rs, d):
-        return remote(ref, buf.at[me_kv], ss.at[d], rs.at[me_kv], at_kv(up(me_kv, d, n_kv)))
-
-    def kv_arrival(ref, buf, ss, rs, d):
-        src = down(me_kv, d, n_kv)
-        return remote(ref, buf.at[src], ss.at[d], rs.at[src], at_kv(src))
+        src = down(me_q, d, n_q)
+        return remote(enc, encbuf.at[me_kv, src], enc_s.at[d], enc_r.at[src], at_q(src))
+
+    def dec_copy(d):
+        mine = dec.at[me_kv, me_q]
+        return remote(mine, mine, dec_s.at[d], dec_r.at[me_q], at_q(up(me_q, d, n_q)))
+
+    def dec_arrival(d):
+        src = down(me_q, d, n_q)
+        part = dec.at[me_kv, src]
+        return remote(part, part, dec_s.at[d], dec_r.at[src], at_q(src))
+
+    def q_copy(block, way):
+        peer = jnp.clip(me_q + way, 0, n_q - 1)
+        return remote(qbuf.at[block], qbuf.at[block], q_s.at[block], q_r.at[block], at_q(peer))
+
+    def own_q(way):
+        peer = jnp.clip(me_q + way, 0, n_q - 1)
+        return remote(qh, qbuf.at[me_q], q_s.at[n_q + int(way > 0)], q_r.at[me_q], at_q(peer))
+
+    def q_step(t):
+        for way in (1, -1):
+            src = me_q - way * t
+            block = jnp.clip(src, 0, n_q - 1)
+
+            @pl.when((src >= 0) & (src < n_q))
+            def _():
+                q_copy(block, -way).wait_recv()
+
+                @pl.when((me_q + way >= 0) & (me_q + way < n_q))
+                def _():
+                    q_copy(block, way).start()
+
+    other = c * LOW + 1 - lo
+
+    def plane(src, buf, ss, rs):
+        def low():
+            return remote(src, buf.at[me_kv], ss.at[0, 0], rs.at[me_kv], at_kv(other))
+
+        def far(d, relay):
+            block = other if relay else me_kv
+            peer = up(c, d, n_coarse) * LOW + lo
+            return remote(buf.at[other] if relay else src, buf.at[block],
+                          ss.at[int(relay), d], rs.at[block], at_kv(peer))
+
+        def arrival(block):
+            return remote(src, buf.at[block], ss.at[0, 0], rs.at[block], at_kv(block))
+
+        def begin():
+            low().start()
+            for d in range(1, n_coarse):
+                far(d, False).start()
+
+        def relay():
+            arrival(other).wait_recv()
+            for d in range(1, n_coarse):
+                far(d, True).start()
+
+        def arrive():
+            for d in range(1, n_coarse):
+                column = up(c, d, n_coarse) * LOW
+                for part in range(LOW):
+                    arrival(column + part).wait_recv()
+
+        def sent():
+            low().wait_send()
+            for d in range(1, n_coarse):
+                far(d, False).wait_send()
+                far(d, True).wait_send()
+
+        return begin, relay, arrive, sent
+
+    enc_plane = plane(encbuf.at[me_kv], encbuf, ek_s, ek_r)
+    dec_plane = plane(dec.at[me_kv], dec, dk_s, dk_r)
+    k_plane = plane(kh, kbuf, k_s, k_r)
+    v_plane = plane(vh, vbuf, v_s, v_r)
 
     def o_copy(d):
         peer = up(me_q, d, n_q)
@@ -117,14 +177,6 @@
             remote(ssend.at[src], srecv.at[src], st_s.at[d], st_r.at[src], at_q(src)),
         )
 
-    def dec_copy(d):
-        peer = up(here, d, n_seq)
-        return remote(dec.at[here], dec.at[here], dec_s.at[d], dec_r.at[here], at_seq(peer))
-
-    def dec_arrival(d):
-        src = down(here, d, n_seq)
-        return remote(dec.at[src], dec.at[src], dec_s.at[d], dec_r.at[src], at_seq(src))
-
     def halo_copy(side):
         peer = jnp.clip(here + 1 - 2 * side, 0, n_seq - 1)
         return (
@@ -138,26 +190,25 @@
             return carry
         lax.fori_loop(start, stop, step, 0)
 
-    loop(1, n_seq, lambda d: enc_copy(d).start())
-    for d in range(1, n_q):
-        q_copy(d).start()
-    for d in range(1, n_kv):
-        kv_copy(kh, kbuf, k_s, k_r, d).start()
-        kv_copy(vh, vbuf, v_s, v_r, d).start()
+    for d in range(1, n_q):
+        enc_copy(d).start()
+    k_plane[0]()
+    v_plane[0]()
+    has_up = me_q < n_q - 1
+    has_down = me_q > 0
+
+    @pl.when(has_up)
+    def _():
+        own_q(1).start()
+
+    @pl.when(has_down)
+    def _():
+        own_q(-1).start()
+
     has_next = here < n_seq - 1
     has_prev = here > 0
 
-    @pl.when(has_next)
-    def _():
-        for copy in halo_copy(0):
-            copy.start()
-
-    @pl.when(has_prev)
-    def _():
-        for copy in halo_copy(1):
-            copy.start()
-
-    encbuf[here] = enc[...]
+    encbuf[me_kv, me_q] = enc[...]
     qbuf[me_q] = qh[...]
     kbuf[me_kv] = kh[...]
     vbuf[me_kv] = vh[...]
@@ -175,7 +226,27 @@
             [jnp.where(lane_d < HEAD, q, 0.0), jnp.where(lane_d < HEAD, swapped, 0.0)], axis=0
         )
         dq[2 * j * dec_rows:(2 * j + 2) * dec_rows, :] = both.astype(jnp.bfloat16)
-    loop(1, n_seq, lambda d: enc_arrival(d).wait_recv())
+    for d in range(1, n_q):
+        enc_arrival(d).wait_recv()
+    enc_plane[0]()
+    q_step(1)
+    enc_plane[1]()
+    k_plane[1]()
+    v_plane[1]()
+
+    @pl.when(has_next)
+    def _():
+        for copy in halo_copy(0):
+            copy.start()
+
+    @pl.when(has_prev)
+    def _():
+        for copy in halo_copy(1):
+            copy.start()
+
+    for t in range(2, n_q - 1):
+        q_step(t)
+    enc_plane[2]()
     d_total = heads * dec_rows
     d_chunk = min(256, d_total)
 
@@ -191,20 +262,25 @@
     for j in range(pairs):
         even = do[2 * j * dec_rows:(2 * j + 1) * dec_rows, :]
         odd = do[(2 * j + 1) * dec_rows:(2 * j + 2) * dec_rows, :]
-        dec[here, :, j * PAIR:(j + 1) * PAIR] = jnp.where(
+        dec[me_kv, me_q, :, j * PAIR:(j + 1) * PAIR] = jnp.where(
             lane_d < HEAD, pltpu.roll(even, HEAD, 1), odd
         ).astype(jnp.bfloat16)
-    loop(1, n_seq, lambda d: dec_copy(d).start())
+    for d in range(1, n_q):
+        dec_copy(d).start()
 
     low_half = lax.broadcasted_iota(jnp.int32, (tokens, PAIR), 1) < HEAD
     lane = lax.broadcasted_iota(jnp.int32, (tokens, PAIR), 1)
-    for d in range(1, n_kv):
-        kv_arrival(kh, kbuf, k_s, k_r, d).wait_recv()
-        kv_arrival(vh, vbuf, v_s, v_r, d).wait_recv()
+    if n_q > 2:
+        q_step(n_q - 1)
+    for d in range(1, n_q):
+        dec_arrival(d).wait_recv()
+    dec_plane[0]()
+    k_plane[2]()
+    v_plane[2]()
     for d in list(range(1, n_q)) + [0]:
         block = up(me_q, d, n_q)
-        if d:
-            q_arrival(d).wait_recv()
+        if d == 0:
+            dec_plane[1]()
 
         def pair_step(j, stat):
             cols = pl.ds(pl.multiple_of(j * PAIR, PAIR), PAIR)
@@ -293,16 +369,30 @@
 
     loop(0, pairs, join_step)
 
-    loop(1, n_seq, lambda d: dec_arrival(d).wait_recv())
-    loop(1, n_seq, lambda d: enc_copy(d).wait_send())
-    loop(1, n_seq, lambda d: dec_copy(d).wait_send())
-    for d in range(1, n_q):
-        q_copy(d).wait_send()
+    dec_plane[2]()
+    for part in (enc_plane, dec_plane, k_plane, v_plane):
+        part[3]()
+    for d in range(1, n_q):
+        enc_copy(d).wait_send()
+        dec_copy(d).wait_send()
         for copy in o_copy(d):
             copy.wait_send()
-    for d in range(1, n_kv):
-        kv_copy(kh, kbuf, k_s, k_r, d).wait_send()
-        kv_copy(vh, vbuf, v_s, v_r, d).wait_send()
+
+    @pl.when(has_up)
+    def _():
+        own_q(1).wait_send()
+
+    @pl.when(has_down)
+    def _():
+        own_q(-1).wait_send()
+
+    for t in range(1, n_q - 1):
+        for way in (1, -1):
+            src = me_q - way * t
+
+            @pl.when((src >= 0) & (src < n_q) & (me_q + way >= 0) & (me_q + way < n_q))
+            def _():
+                q_copy(jnp.clip(src, 0, n_q - 1), way).wait_send()
 
     @pl.when(has_next)
     def _():
@@ -327,8 +417,9 @@
     heads = width // HEAD
     count = dec_queries.shape[1]
     dec_rows = count // n_seq
-    here = lax.axis_index(("coarse", "fine"))
-    mine = lax.dynamic_slice_in_dim(dec_queries.reshape(n_seq, dec_rows, width), here, 1)
+    fine = lax.axis_index("fine")
+    slot = (lax.axis_index("coarse") * LOW + fine % LOW) * n_q + fine // LOW
+    mine = lax.dynamic_slice_in_dim(dec_queries.reshape(n_seq, dec_rows, width), slot, 1)
     args = [q_light[0], k_light[0], v_light[0], q_heavy[0], k_heavy[0], v_heavy[0], enc_kv[0], mine]
     has_bias = key_ids.shape[1] != n_seq
     if has_bias:
@@ -345,12 +436,12 @@
         functools.partial(kernel, (n_coarse, n_fine, tokens, width, dec_rows), has_bias),
         out_shape=(
             jax.ShapeDtypeStruct((tokens, width), bf16),
-            jax.ShapeDtypeStruct((n_seq, dec_rows, width), bf16),
+            jax.ShapeDtypeStruct((n_kv, n_q, dec_rows, width), bf16),
         ),
         in_specs=[vmem] * len(args),
         out_specs=(vmem, vmem),
         scratch_shapes=[
-            pltpu.VMEM((n_seq, tokens, PAIR), bf16),
+            pltpu.VMEM((n_kv, n_q, tokens, PAIR), bf16),
             pltpu.VMEM((heads * dec_rows, PAIR), bf16),
             pltpu.VMEM((heads * dec_rows, PAIR), f32),
             pltpu.VMEM((n_q, tokens, width), bf16),
@@ -365,14 +456,16 @@
             pltpu.VMEM((n_q, tokens, PAIR), f32),
             pltpu.VMEM((tokens, width), f32),
             pltpu.VMEM((tokens, 3 * tokens), f32),
-            dma((n_seq,)), dma((n_seq,)),
-            dma((n_seq,)), dma((n_seq,)),
             dma((n_q,)), dma((n_q,)),
-            dma((n_kv,)), dma((n_kv,)),
-            dma((n_kv,)), dma((n_kv,)),
+            dma((n_q,)), dma((n_q,)),
+            dma((n_q + 2,)), dma((n_q,)),
             dma((n_q,)), dma((n_q,)),
             dma((n_q,)), dma((n_q,)),
             dma((2, 2)), dma((2, 2)),
+            dma((2, n_coarse)), dma((n_kv,)),
+            dma((2, n_coarse)), dma((n_kv,)),
+            dma((2, n_coarse)), dma((n_kv,)),
+            dma((2, n_coarse)), dma((n_kv,)),
         ],
         compiler_params=pltpu.CompilerParams(
             collective_id=0, has_side_effects=True, vmem_limit_bytes=60 * 1024 * 1024

time: 111 us -> 83.8 us (0.75)
  the two profiles are of different devices: /device:TPU:10 before, /device:TPU:15 now
where the time goes in v2:
time: 83.8 us; the launch traced here: 83.6 us
  Pallas kernels  77.1 us (92%)
  local copies, waits for them, and re-layouts  5.76 us (7%)
    pallas_call x1, Pallas kernels, local(): pl.pallas_call(functools.partial(kernel, (n_coarse, n_fine, tokens, width...  77.1 us
    unnamed x4, local copies, waits for them, and re-layouts  5.13 us

profile of v2, /device:TPU:15, one launch (start us, length us, event | category | flops | bytes accessed | tf_op | source)
XLA Modules:
  0.0 83.6 jit_solution(1908085324006060886)
XLA Ops:
  0.6 0.0 copy-start
  0.7 1.2 %copy-done = bf16[1,512,1024]{2,1,0:T(8,128)(2,1)S(1)} copy-done((bf16[1,512,1024]{2,1,0:T(8,128)(2,1)S(1)}, bf16[1,512,1024]{2,1,0:T(8,128)(2,1)}, u32[]{:S(2)}) %copy-start) | copy-done | bytes 1048600
  1.9 0.6 constant_dynamic-slice_fusion.refs_7_
  2.5 77.1 %shard_map.95 = (bf16[128,1024]{1,0:T(8,128)(2,1)}, bf16[4,4,32,1024]{3,2,1,0:T(8,128)(2,1)}) custom-call(bf16[128,1024]{1,0:T(8,128)(2,1)} %bitcast.12, bf16[128,1024]{1,0:T(8,128)(2,1)} %bitcast.13, bf16[128,1024]{1,0:T(8,128)(2,1)} %bitcast.14, bf16[128,1024]{1,0:T(8,128)(2,1)} %bitcast.15, bf16[128,1024]{1,0:T(8,128)(2,1)} %bitcast.16, ...), custom_call_target="tpu_custom_call" | custom-call | tf_op jit(solution)/shard_map/pallas_call | solution.py:435
  79.6 1.7 %copy.12 = bf16[1,128,1024]{2,1,0:T(8,128)(2,1)} copy(bf16[1,128,1024]{2,1,0:T(8,128)(2,1)} %bitcast.18) | data formatting | bytes 524288
  81.3 2.3 %copy.13 = bf16[1,512,1024]{2,1,0:T(8,128)(2,1)} copy(bf16[1,512,1024]{2,1,0:T(8,128)(2,1)} %bitcast.11) | data formatting | bytes 2097152
Async XLA Ops:
  0.6 1.2 %copy-start = (bf16[1,512,1024]{2,1,0:T(8,128)(2,1)S(1)}, bf16[1,512,1024]{2,1,0:T(8,128)(2,1)}, u32[]{:S(2)}) copy-start(bf16[1,512,1024]{2,1,0:T(8,128)(2,1)} %param.17) | copy-start | bytes 3145732

commit v3 on v2

--- a/solution.py
+++ b/solution.py
@@ -42,7 +42,7 @@
     bias_ref = refs[8] if has_bias else None
     (out, dec, encbuf, dq, do, qbuf, kbuf, vbuf, khalo, vhalo, osend, orecv, ssend, srecv,
      wts, light, band, enc_s, enc_r, dec_s, dec_r, q_s, q_r, o_s, o_r, st_s, st_r, h_s, h_r,
-     ek_s, ek_r, dk_s, dk_r, k_s, k_r, v_s, v_r) = refs[8 + has_bias:]
+     ek_s, ek_r, dk_s, dk_r, k_s, k_r, v_s, v_r, drows, load_s) = refs[8 + has_bias:]
 
     c = lax.axis_index("coarse")
     f = lax.axis_index("fine")
@@ -72,6 +72,8 @@
     def down(me, d, n):
         return lax.rem(me + n - d, n)
 
+    load = pltpu.make_async_copy(decq.at[me_kv, me_q], drows, load_s)
+    load.start()
     barrier = pltpu.get_barrier_semaphore()
 
     def greet(d, carry):
@@ -193,7 +195,6 @@
     for d in range(1, n_q):
         enc_copy(d).start()
     k_plane[0]()
-    v_plane[0]()
     has_up = me_q < n_q - 1
     has_down = me_q > 0
 
@@ -209,6 +210,21 @@
     has_prev = here > 0
 
     encbuf[me_kv, me_q] = enc[...]
+    for d in range(1, n_q):
+        enc_arrival(d).wait_recv()
+    enc_plane[0]()
+    v_plane[0]()
+
+    @pl.when(has_next)
+    def _():
+        for copy in halo_copy(0):
+            copy.start()
+
+    @pl.when(has_prev)
+    def _():
+        for copy in halo_copy(1):
+            copy.start()
+
     qbuf[me_q] = qh[...]
     kbuf[me_kv] = kh[...]
     vbuf[me_kv] = vh[...]
@@ -218,31 +234,19 @@
     seen = (jnp.abs(col - tokens - row) <= ROUTED_BLOCK - 1) & (pos >= 0) & (pos < n_seq * tokens)
     band[...] = jnp.where(seen, jnp.float32(0), jnp.float32(NEG))
 
+    load.wait()
     lane_d = lax.broadcasted_iota(jnp.int32, (dec_rows, PAIR), 1)
     for j in range(pairs):
-        q = decq[0, :, j * PAIR:(j + 1) * PAIR].astype(jnp.float32) * (HEAD ** (-0.5))
+        q = drows[:, j * PAIR:(j + 1) * PAIR].astype(jnp.float32) * (HEAD ** (-0.5))
         swapped = pltpu.roll(q, HEAD, 1)
         both = jnp.concatenate(
             [jnp.where(lane_d < HEAD, q, 0.0), jnp.where(lane_d < HEAD, swapped, 0.0)], axis=0
         )
         dq[2 * j * dec_rows:(2 * j + 2) * dec_rows, :] = both.astype(jnp.bfloat16)
-    for d in range(1, n_q):
-        enc_arrival(d).wait_recv()
-    enc_plane[0]()
     q_step(1)
     enc_plane[1]()
     k_plane[1]()
     v_plane[1]()
-
-    @pl.when(has_next)
-    def _():
-        for copy in halo_copy(0):
-            copy.start()
-
-    @pl.when(has_prev)
-    def _():
-        for copy in halo_copy(1):
-            copy.start()
 
     for t in range(2, n_q - 1):
         q_step(t)
@@ -417,9 +421,7 @@
     heads = width // HEAD
     count = dec_queries.shape[1]
     dec_rows = count // n_seq
-    fine = lax.axis_index("fine")
-    slot = (lax.axis_index("coarse") * LOW + fine % LOW) * n_q + fine // LOW
-    mine = lax.dynamic_slice_in_dim(dec_queries.reshape(n_seq, dec_rows, width), slot, 1)
+    mine = dec_queries.reshape(n_kv, n_q, dec_rows, width)
     args = [q_light[0], k_light[0], v_light[0], q_heavy[0], k_heavy[0], v_heavy[0], enc_kv[0], mine]
     has_bias = key_ids.shape[1] != n_seq
     if has_bias:
@@ -438,7 +440,7 @@
             jax.ShapeDtypeStruct((tokens, width), bf16),
             jax.ShapeDtypeStruct((n_kv, n_q, dec_rows, width), bf16),
         ),
-        in_specs=[vmem] * len(args),
+        in_specs=[vmem] * 7 + [pl.BlockSpec(memory_space=pl.ANY)] + [vmem] * (len(args) - 8),
         out_specs=(vmem, vmem),
         scratch_shapes=[
             pltpu.VMEM((n_kv, n_q, tokens, PAIR), bf16),
@@ -466,6 +468,7 @@
             dma((2, n_coarse)), dma((n_kv,)),
             dma((2, n_coarse)), dma((n_kv,)),
             dma((2, n_coarse)), dma((n_kv,)),
+            pltpu.VMEM((dec_rows, width), bf16), dma,
         ],
         compiler_params=pltpu.CompilerParams(
             collective_id=0, has_side_effects=True, vmem_limit_bytes=60 * 1024 * 1024

time: 83.8 us -> 79.5 us (0.949)
  the two profiles are of different devices: /device:TPU:15 before, /device:TPU:10 now
where the time goes in v3:
time: 79.5 us; the launch traced here: 79.2 us
  Pallas kernels  74.7 us (94%)
  local copies, waits for them, and re-layouts  3.93 us (5%)
    pallas_call x1, Pallas kernels, local(): pl.pallas_call(functools.partial(kernel, (n_coarse, n_fine, tokens, width...  74.7 us
    unnamed x2, local copies, waits for them, and re-layouts  3.93 us

profile of v3, /device:TPU:10, one launch (start us, length us, event | category | flops | bytes accessed | tf_op | source)
XLA Modules:
  0.0 79.2 jit_solution(11207994403442865562)
XLA Ops:
  0.6 74.7 %shard_map.95 = (bf16[128,1024]{1,0:T(8,128)(2,1)}, bf16[4,4,32,1024]{3,2,1,0:T(8,128)(2,1)}) custom-call(bf16[128,1024]{1,0:T(8,128)(2,1)} %bitcast.13, bf16[128,1024]{1,0:T(8,128)(2,1)} %bitcast.14, bf16[128,1024]{1,0:T(8,128)(2,1)} %bitcast.15, bf16[128,1024]{1,0:T(8,128)(2,1)} %bitcast.16, bf16[128,1024]{1,0:T(8,128)(2,1)} %bitcast.17, ...), custom_call_target="tpu_custom_call" | custom-call | tf_op jit(solution)/shard_map/pallas_call | solution.py:437
  75.3 1.7 %copy.12 = bf16[1,128,1024]{2,1,0:T(8,128)(2,1)} copy(bf16[1,128,1024]{2,1,0:T(8,128)(2,1)} %bitcast.12) | data formatting | bytes 524288
  77.0 2.3 %copy.13 = bf16[1,512,1024]{2,1,0:T(8,128)(2,1)} copy(bf16[1,512,1024]{2,1,0:T(8,128)(2,1)} %bitcast.10) | data formatting | bytes 2097152
